TPU v7x, 256 devices: a whole 4x4x8 slice. The times are simulated.
256 devices in a mesh: mic: 4 (over y), seq: 64 (over z, x, core).
Axes of the slice: x: 4, y: 4, z: 8, core: 2. Of those that a mesh axis runs over, the one named last changes fastest.
Arguments:
- frames_in: bfloat16 [8, 32768, 512], P('mic', 'seq'), may hold values from -16 to 16
- w_qkv: bfloat16 [8, 512, 1536], P('mic'), may hold values from -0.25 to 0.25
- w_join: bfloat16 [4096, 1024], P(('mic', 'seq')), may hold values from -0.09375 to 0.09375
- norm_gain: float32 [1024], replicated, may hold values from 0.5 to 2
- w_router: bfloat16 [1024, 64], replicated, may hold values from -0.1875 to 0.1875
- w_gate: bfloat16 [64, 1024, 4096], P('seq', None, 'mic'), may hold values from -0.1875 to 0.1875
- w_up: bfloat16 [64, 1024, 4096], P('seq', None, 'mic'), may hold values from -0.1875 to 0.1875
- w_down: bfloat16 [64, 4096, 1024], P('seq', 'mic'), may hold values from -0.09375 to 0.09375
- expert_ids: int32 [64, 4, 128, 2], P('seq', 'mic'), may hold values from 0 to 63, all different within a row; in each aligned block of 128 rows (0 to 127, 128 to 255, ..., all dimensions but the last counted through in order) at most 6 rows name the same one
Outputs:
- layer_out: bfloat16 [64, 4, 128, 1024], P('seq', 'mic')
Inputs may be any that keep to these rules, and one draw needn't show every extreme that they name: `expert_ids`: in the rows of one block (128 frames) no expert is named more than 6 times, a bound that some block reaches; the two ids of a frame differ.
All inputs are finite; a program needn't handle non-finite values.
Results may differ from a plain program's by a relative error of at most 0.017.
Values may be sent and summed in bfloat16 or wider, within the bound.
A program may use at most 128 MiB of HBM per device.

v0:
```python
import jax
import jax.numpy as jnp
from jax import lax
from jax.sharding import PartitionSpec as P

MICS = 8
HEADS = 8
TOP = 2


def body(frames_in, w_qkv, w_join, norm_gain, w_router, w_gate, w_up, w_down, expert_ids):
    mic_count = lax.axis_size("mic")
    seq_count = lax.axis_size("seq")
    mic_local, span, chan_width = frames_in.shape
    frame_rows = span // mic_count
    head_dim = chan_width // HEADS
    model_width = w_join.shape[1]
    expert_count = w_router.shape[1]
    exp_local = w_gate.shape[0]
    capacity = max(2, 3 * TOP * frame_rows // (2 * expert_count))
    projected = jnp.einsum(
        "mfc,mce->mfe", frames_in, w_qkv, preferred_element_type=jnp.float32
    ).astype(jnp.bfloat16)
    projected = projected.reshape(mic_local, mic_count, frame_rows, 3 * chan_width)
    arrived_block = lax.all_to_all(projected, "mic", split_axis=1, concat_axis=0, tiled=True)
    arrived_block = arrived_block[:, 0]
    frame_count = arrived_block.shape[1]
    queries = arrived_block[..., :chan_width].reshape(MICS, frame_count, HEADS, head_dim)
    keys_all = arrived_block[..., chan_width : 2 * chan_width].reshape(
        MICS, frame_count, HEADS, head_dim
    )
    values_all = arrived_block[..., 2 * chan_width :].reshape(MICS, frame_count, HEADS, head_dim)
    scores = jnp.einsum(
        "ifhd,jfhd->fhij", queries, keys_all, preferred_element_type=jnp.float32
    ) * head_dim ** (-0.5)
    row_max = jnp.max(scores, axis=-1, keepdims=True)
    weights = jnp.exp(scores - row_max)
    probs = (weights / jnp.sum(weights, axis=-1, keepdims=True)).astype(jnp.bfloat16)
    mixed_heads = jnp.einsum(
        "fhij,jfhd->fihd", probs, values_all, preferred_element_type=jnp.float32
    )
    attended = mixed_heads.astype(jnp.bfloat16).reshape(frame_count, MICS * chan_width)
    joined = jnp.dot(
        attended,
        lax.all_gather(w_join, ("mic", "seq"), axis=0, tiled=True),
        preferred_element_type=jnp.float32,
    )
    scale_row = lax.rsqrt(jnp.mean(joined * joined, axis=-1, keepdims=True) + 1e-06)
    normed = (joined * scale_row * norm_gain).astype(jnp.bfloat16)
    logits = jnp.dot(normed, w_router, preferred_element_type=jnp.float32)
    expert_rows = expert_ids.reshape(frame_rows, TOP)
    chosen = (expert_rows[..., None] == jnp.arange(expert_count, dtype=jnp.int32)).astype(jnp.int32)
    picked = jnp.sum(logits[:, None, :] * chosen.astype(jnp.float32), axis=-1)
    first_gate = 1.0 / (1.0 + jnp.exp(picked[:, 1] - picked[:, 0]))
    gates = jnp.stack([first_gate, 1.0 - first_gate], axis=-1)
    counts = jnp.sum(chosen, axis=1)
    before = jnp.cumsum(counts, axis=0) - counts
    slot_index = jnp.sum(before[:, None, :] * chosen, axis=-1)
    in_slot = slot_index[..., None] == jnp.arange(capacity, dtype=jnp.int32)
    mapped = (
        ((chosen[..., :, None] == 1) & in_slot[..., None, :])
        .reshape(frame_rows, TOP, expert_count * capacity)
        .astype(jnp.bfloat16)
    )
    merged_map = jnp.sum(mapped, axis=1)
    buffers = jnp.einsum(
        "rs,rd->sd", merged_map, normed, preferred_element_type=jnp.float32
    ).astype(jnp.bfloat16)
    buffers = buffers.reshape(seq_count, exp_local * capacity, model_width)
    landed = lax.all_to_all(buffers, "seq", split_axis=0, concat_axis=0, tiled=True)
    arrived = lax.all_gather(landed[None], "mic", axis=0, tiled=True)
    flat = arrived.reshape(mic_count * seq_count * exp_local * capacity, model_width)
    piece_rows = flat.reshape(-1, exp_local, capacity, model_width)
    first_proj = jnp.einsum(
        "nejd,edf->nejf", piece_rows, w_gate, preferred_element_type=jnp.float32
    )
    second_proj = jnp.einsum("nejd,edf->nejf", piece_rows, w_up, preferred_element_type=jnp.float32)
    inner = (jax.nn.silu(first_proj) * second_proj).astype(jnp.bfloat16)
    result = jnp.einsum("nejf,efd->nejd", inner, w_down, preferred_element_type=jnp.float32)
    summed = lax.psum_scatter(
        result.reshape(
            lax.axis_size("mic") * (seq_count * exp_local * capacity), model_width
        ).astype(jnp.bfloat16),
        "mic",
        scatter_dimension=0,
        tiled=True,
    ).astype(jnp.float32)
    summed = summed.astype(jnp.bfloat16).reshape(seq_count, exp_local * capacity, model_width)
    returned = lax.all_to_all(summed, "seq", split_axis=0, concat_axis=0, tiled=True)
    returned = returned.reshape(expert_count * capacity, model_width)
    picked_out = jnp.einsum("rks,sd->rkd", mapped, returned, preferred_element_type=jnp.float32)
    total = joined + jnp.sum(gates[..., None] * picked_out, axis=1)
    return total.astype(jnp.bfloat16).reshape(1, 1, frame_rows, model_width)


def solution(mesh):
    return jax.shard_map(
        body,
        mesh=mesh,
        in_specs=(
            P("mic", "seq", None),
            P("mic", None, None),
            P(("mic", "seq"), None),
            P(),
            P(),
            P("seq", None, "mic"),
            P("seq", None, "mic"),
            P("seq", "mic", None),
            P("seq", "mic", None, None),
        ),
        out_specs=P("seq", "mic", None, None),
        check_vma=False,
    )
```

profile of v0, /device:TPU:1, one launch (start us, length us, event | category | flops | bytes accessed | tf_op | source)
XLA Modules:
  0.0 346.4 jit_solution(7928431488291336185)
XLA Ops:
  6.5 0.0 copy-start
  6.5 0.0 all-gather.4.cloned.1.call-start
  6.5 0.7 all-gather.4.cloned.1.call-update
  7.3 1.2 copy-done
  8.4 3.0 convolution_convert_fusion
  11.5 2.0 copy.26
  13.4 0.0 copy-start.8
  13.4 5.1 %all-to-all-start = ((bf16[2,4,128,1536]{3,2,0,1:T(8,128)(2,1)}), bf16[2,4,128,1536]{3,2,0,1:T(8,128)(2,1)S(1)}, u32[]{:S(2)}, u32[]{:S(2)}) async-start(bf16[2,4,128,1536]{3,2,0,1:T(8,128)(2,1)} %copy.26), calls=%async_computation | async-start | bytes 6291456 | tf_op jit(solution)/shard_map/all_to_all | solution.py:25
  18.6 0.0 all-gather.6.cloned.1.call-start
  18.6 0.0 copy-done.8
  18.6 0.1 copy.35
  18.7 0.2 reduce_window_sum.11
  18.9 0.1 copy.37
  19.1 0.1 copy.38
  19.2 35.4 %all-to-all-done = bf16[2,4,128,1536]{3,2,0,1:T(8,128)(2,1)S(1)} async-done(((bf16[2,4,128,1536]{3,2,0,1:T(8,128)(2,1)}), bf16[2,4,128,1536]{3,2,0,1:T(8,128)(2,1)S(1)}, u32[]{:S(2)}, u32[]{:S(2)}) %all-to-all-start) | async-done | bytes 3145760 | tf_op jit(solution)/shard_map/all_to_all | solution.py:25
  54.6 1.7 fusion.37
  56.4 0.0 copy-start.4
  56.4 1.7 copy.28
  58.1 3.8 %copy.30 = bf16[8,128,8,64]{3,0,2,1:T(8,128)(2,1)} copy(bf16[8,128,8,64]{1,3,2,0:T(8,128)(2,1)S(1)} %bitcast.103) | data formatting | bytes 2097152 | tf_op jit(solution)/shard_map/reshape | solution.py:28
  61.8 0.0 copy-start.3
  61.8 0.0 copy-done.4
  61.8 0.7 copy.29
  62.5 3.7 %copy.31 = bf16[8,128,8,64]{3,0,2,1:T(8,128)(2,1)} copy(bf16[8,128,8,64]{1,3,2,0:T(8,128)(2,1)S(1)} %bitcast.104) | data formatting | bytes 2097152 | tf_op jit(solution)/shard_map/reshape | solution.py:29
  66.2 0.0 copy-done.3
  66.2 0.7 copy.27
  66.9 0.0 copy-start.5
  66.9 3.7 %copy.32 = bf16[8,128,8,64]{3,0,2,1:T(8,128)(2,1)} copy(bf16[8,128,8,64]{1,3,2,0:T(8,128)(2,1)S(1)} %bitcast.105) | data formatting | bytes 2097152 | tf_op jit(solution)/shard_map/reshape | solution.py:32
  70.6 0.0 copy-done.5
  70.6 6.6 %fusion.38 = (f32[128,8,8]{2,1,0:T(8,128)S(1)}, f32[128,8,8,8]{2,3,1,0:T(8,128)}) fusion(bf16[8,128,8,64]{3,0,2,1:T(8,128)(2,1)S(1)} %copy-done.5, bf16[8,128,8,64]{3,0,2,1:T(8,128)(2,1)} %copy.31), kind=kOutput, calls=%fused_computation.56 | convolution fusion | flops 8585223 | bytes 2392064 | tf_op jit(solution)/shard_map/sub | solution.py:37
  77.2 4.7 %convert_bitcast_fusion.1 = bf16[128,8,8,64]{3,1,2,0:T(8,128)(2,1)} fusion(bf16[8,128,8,64]{3,0,2,1:T(8,128)(2,1)} %copy.32, f32[128,8,8,8]{2,3,1,0:T(8,128)} %get-tuple-element.11, f32[128,8,8]{2,1,0:T(8,128)S(1)} %get-tuple-element.10), kind=kOutput, calls=%fused_computation.22 | convolution fusion | flops 9043968 | bytes 2392064 | tf_op jit(solution)/shard_map/fhij,jfhd->fihd/dot_general | solution.py:39
  81.9 3.2 copy.34
  85.1 59.5 %all-gather.4.cloned.1.call-done = bf16[4096,1024]{1,0:T(8,128)(2,1)} async-done(((bf16[16,1024]{1,0:T(8,128)(2,1)}), bf16[4096,1024]{1,0:T(8,128)(2,1)}) %all-gather.4.cloned.1.call-update) | async-done | bytes 8388624 | tf_op jit(solution)/shard_map/all_gather | solution.py:45
  144.6 0.0 copy-start.7
  144.6 4.7 %multiply_reduce_fusion.1 = (f32[128]{0:T(128)S(1)}, f32[128,1024]{1,0:T(8,128)S(1)}) fusion(bf16[128,4096]{0,1:T(8,128)(2,1)S(1)} %bitcast.102, bf16[4096,1024]{1,0:T(8,128)(2,1)} %all-gather.4.cloned.1.call-done), kind=kOutput, calls=%fused_computation.33 | convolution fusion | flops 1074003840 | bytes 9961984 | tf_op jit(solution)/shard_map/dot_general | solution.py:43
  149.3 0.0 copy-start.2
  149.3 0.0 copy-done.7
  149.3 0.4 convolution_convert_fusion.1
  149.8 0.3 reshape.92
  150.0 35.1 %all_to_all.25 = bf16[64,6,1024]{2,1,0:T(8,128)(2,1)S(1)} all-to-all(bf16[64,6,1024]{2,1,0:T(8,128)(2,1)S(1)} %reshape.92), channel_id=1, replica_groups=mesh['mic'=4,'seq'=64] {'seq'}, dimensions={0} | all-to-all | bytes 1572864 | tf_op jit(solution)/shard_map/all_to_all | solution.py:70
  185.1 1.3 copy.39
  186.4 0.0 copy-done.2
  186.4 0.0 all-gather.6.cloned.1.call-update
  186.5 0.0 reduce-scatter.2.cloned.1.call-start
  186.5 37.7 %all-gather.6.cloned.1.call-done = bf16[256,6,1024]{2,0,1:T(8,128)(2,1)} async-done(((bf16[64,6,1024]{2,0,1:T(8,128)(2,1)}), bf16[256,6,1024]{2,0,1:T(8,128)(2,1)}) %all-gather.6.cloned.1.call-update) | async-done | bytes 3145744 | tf_op jit(solution)/shard_map/all_gather | solution.py:71
  224.2 8.6 %fusion.19 = f32[256,6,1024]{2,0,1:T(8,128)} fusion(bf16[256,6,1024]{2,0,1:T(8,128)(2,1)} %all-gather.6.cloned.1.call-done, bf16[1,1024,1024]{2,1,0:T(8,128)(2,1)} %param.14), kind=kOutput, calls=%fused_computation.20 | convolution fusion | flops 3221225472 | bytes 11534336 | tf_op jit(solution)/shard_map/nejd,edf->nejf/dot_general | solution.py:74
  232.8 10.6 %convert_bitcast_fusion = bf16[256,1,6,1024]{3,0,2,1:T(8,128)(2,1)S(1)} fusion(f32[256,6,1024]{2,0,1:T(8,128)} %fusion.19, bf16[256,6,1024]{2,0,1:T(8,128)(2,1)} %all-gather.6.cloned.1.call-done, bf16[1,1024,1024]{2,1,0:T(8,128)(2,1)} %param.16, bf16[1,1024,1024]{2,1,0:T(8,128)(2,1)} %param.15), kind=kOutput, calls=%fused_computation.15 | convolution fusion | flops 6453460992 | bytes 16777216 | tf_op jit(solution)/shard_map/nejf,efd->nejd/dot_general | solution.py:79
  243.4 3.7 %copy.40 = bf16[256,1,6,1024]{3,2,0,1:T(8,128)(2,1)} copy(bf16[256,1,6,1024]{3,0,2,1:T(8,128)(2,1)S(1)} %convert_bitcast_fusion) | data formatting | bytes 6291456 | tf_op jit(solution)/shard_map/convert_element_type | solution.py:83
  247.1 6.3 %convert_element_type.71 = bf16[1536,1024]{1,0:T(8,128)(2,1)} reshape(bf16[256,1,6,1024]{3,2,0,1:T(8,128)(2,1)} %copy.40) | data formatting | bytes 6291456 | tf_op jit(solution)/shard_map/convert_element_type | solution.py:83
  253.4 0.0 copy-start.6
  253.4 0.0 reduce-scatter.2.cloned.1.call-update
  253.5 41.3 %reduce-scatter.2.cloned.1.call-done = bf16[384,1024]{1,0:T(8,128)(2,1)} async-done(((bf16[1536,1024]{1,0:T(8,128)(2,1)}), bf16[384,1024]{1,0:T(8,128)(2,1)}) %reduce-scatter.2.cloned.1.call-update) | async-done | bytes 786448 | tf_op jit(solution)/shard_map/reduce_scatter | solution.py:80
  294.7 0.0 copy-start.1
  294.7 2.3 reshape.98
  297.1 10.8 %all-to-all-start.2 = ((bf16[64,6,1024]{2,1,0:T(8,128)(2,1)}), bf16[64,6,1024]{2,1,0:T(8,128)(2,1)}, u32[]{:S(2)}, u32[]{:S(2)}) async-start(bf16[64,6,1024]{2,1,0:T(8,128)(2,1)} %reshape.98), calls=%async_computation.3 | async-start | bytes 2097152 | tf_op jit(solution)/shard_map/all_to_all | solution.py:89
  307.9 0.0 copy-done.6
  307.9 1.3 fusion.36
  309.3 26.5 %all-to-all-done.2 = bf16[64,6,1024]{2,1,0:T(8,128)(2,1)} async-done(((bf16[64,6,1024]{2,1,0:T(8,128)(2,1)}), bf16[64,6,1024]{2,1,0:T(8,128)(2,1)}, u32[]{:S(2)}, u32[]{:S(2)}) %all-to-all-start.2) | async-done | bytes 786464 | tf_op jit(solution)/shard_map/all_to_all | solution.py:89
  335.8 2.3 fusion.24
  338.1 1.8 fusion.28
  339.9 0.0 copy-done.1
  (11 shorter events, 0.2 us)
Async XLA Ops:
  6.5 1.9 copy-start
  6.5 138.0 %all-gather.4.cloned.1.call-start = ((), (), s32[]{:S(2)}) async-start(), calls=%async_computation.4 | async-start | bytes 8421376 | tf_op jit(solution)/shard_map/all_gather | solution.py:45
  13.4 5.2 %copy-start.8 = (s32[1,1,128,2]{2,3,1,0:T(2,128)S(1)}, s32[1,1,128,2]{2,3,1,0:T(2,128)}, u32[]{:S(2)}) copy-start(s32[1,1,128,2]{2,3,1,0:T(2,128)} %param.17) | copy-start | bytes 3076
  13.4 41.2 %all-to-all-start = ((bf16[2,4,128,1536]{3,2,0,1:T(8,128)(2,1)}), bf16[2,4,128,1536]{3,2,0,1:T(8,128)(2,1)S(1)}, u32[]{:S(2)}, u32[]{:S(2)}) async-start(bf16[2,4,128,1536]{3,2,0,1:T(8,128)(2,1)} %copy.26), calls=%async_computation | async-start | bytes 6291456 | tf_op jit(solution)/shard_map/all_to_all | solution.py:25
  18.6 205.6 %all-gather.6.cloned.1.call-start = ((), (), s32[]{:S(2)}) async-start(), calls=%async_computation.6 | async-start | bytes 3932160 | tf_op jit(solution)/shard_map/all_gather | solution.py:71
  56.4 5.5 %copy-start.4 = (bf16[8,128,512]{2,1,0:T(8,128)(2,1)S(1)}, bf16[8,128,512]{2,1,0:T(8,128)(2,1)}, u32[]{:S(2)}) copy-start(bf16[8,128,512]{2,1,0:T(8,128)(2,1)} %get-tuple-element.7) | copy-start | bytes 3145732
  61.8 4.4 %copy-start.3 = (bf16[8,128,512]{2,1,0:T(8,128)(2,1)S(1)}, bf16[8,128,512]{2,1,0:T(8,128)(2,1)}, u32[]{:S(2)}) copy-start(bf16[8,128,512]{2,1,0:T(8,128)(2,1)} %get-tuple-element.9) | copy-start | bytes 3145732
  66.9 3.8 %copy-start.5 = (bf16[8,128,8,64]{3,0,2,1:T(8,128)(2,1)S(1)}, bf16[8,128,8,64]{3,0,2,1:T(8,128)(2,1)}, u32[]{:S(2)}) copy-start(bf16[8,128,8,64]{3,0,2,1:T(8,128)(2,1)} %copy.30) | copy-start | bytes 3145732
  144.6 4.8 %copy-start.7 = (f32[1024]{0:T(1024)S(1)}, f32[1024]{0:T(1024)}, u32[]{:S(2)}) copy-start(f32[1024]{0:T(1024)} %param.12) | copy-start | bytes 12292
  149.3 37.1 %copy-start.2 = (f32[128,1024]{1,0:T(8,128)}, f32[128,1024]{1,0:T(8,128)S(1)}, u32[]{:S(2)}) copy-start(f32[128,1024]{1,0:T(8,128)S(1)} %get-tuple-element.13) | copy-start | bytes 1572868
  186.5 108.3 %reduce-scatter.2.cloned.1.call-start = ((), (), s32[]{:S(2)}) async-start(), calls=%async_computation.5 | async-start | bytes 3932160 | tf_op jit(solution)/shard_map/reduce_scatter | solution.py:80
  253.4 54.4 %copy-start.6 = (bf16[1024,64]{0,1:T(8,128)(2,1)S(1)}, bf16[1024,64]{0,1:T(8,128)(2,1)}, u32[]{:S(2)}) copy-start(bf16[1024,64]{0,1:T(8,128)(2,1)} %param.13) | copy-start | bytes 393220
  294.7 45.2 %copy-start.1 = (bf16[2,512,1536]{2,1,0:T(8,128)(2,1)S(1)}, bf16[2,512,1536]{2,1,0:T(8,128)(2,1)}, u32[]{:S(2)}) copy-start(bf16[2,512,1536]{2,1,0:T(8,128)(2,1)} %param.10) | copy-start | bytes 9437188
  297.1 38.7 %all-to-all-start.2 = ((bf16[64,6,1024]{2,1,0:T(8,128)(2,1)}), bf16[64,6,1024]{2,1,0:T(8,128)(2,1)}, u32[]{:S(2)}, u32[]{:S(2)}) async-start(bf16[64,6,1024]{2,1,0:T(8,128)(2,1)} %reshape.98), calls=%async_computation.3 | async-start | bytes 2097152 | tf_op jit(solution)/shard_map/all_to_all | solution.py:89
Sparse Core Ops, SparseCore 0:
  10.9 133.5 all-gather.3
  186.6 37.5 all-gather.5
  253.6 41.0 reduce-scatter.1
where the time goes:
time: 347 us; the launch traced here: 346 us
  waiting for transfers between devices  201 us (58%)
  matrix products  42.3 us (12%)
  local copies, waits for them, and re-layouts  36.6 us (11%)
  blocking collectives  35.1 us (10%)
  starting transfers between devices  16 us (5%)
  between operations  13.3 us (4%)
    all_gather x1, waiting for transfers between devices, body(): lax.all_gather(w_join, ('mic', 'seq'), axis=0, tiled=True)  59.5 us
    reduce_scatter x1, waiting for transfers between devices, body(): lax.psum_scatter(result.reshape(lax.axis_size('mic') * (seq_count * exp_l...  41.3 us
    all_gather x1, waiting for transfers between devices, body(): arrived = lax.all_gather(landed[None], 'mic', axis=0, tiled=True)  37.7 us
    all_to_all x1, waiting for transfers between devices, body(): lax.all_to_all(projected, 'mic', split_axis=1, concat_axis=0, tiled=True)  35.4 us
    all_to_all x1, blocking collectives, body(): lax.all_to_all(buffers, 'seq', split_axis=0, concat_axis=0, tiled=True)  35.1 us
    all_to_all x1, waiting for transfers between devices, body(): lax.all_to_all(summed, 'seq', split_axis=0, concat_axis=0, tiled=True)  26.5 us
    all_to_all x1, starting transfers between devices, body(): lax.all_to_all(summed, 'seq', split_axis=0, concat_axis=0, tiled=True)  10.8 us
    dot_general x1, matrix products, body(): jnp.einsum('nejf,efd->nejd', inner, w_down, preferred_element_type=jnp.fl...  10.6 us
  transfers between devices with their start and end apart: 5, of which 5 were waited for; matrix products, arithmetic and copies ran while one was open for 11% of the time, Pallas kernels for 0%

commit v1 on v0

--- a/solution.py
+++ b/solution.py
@@ -68,7 +68,15 @@
     ).astype(jnp.bfloat16)
     buffers = buffers.reshape(seq_count, exp_local * capacity, model_width)
     landed = lax.all_to_all(buffers, "seq", split_axis=0, concat_axis=0, tiled=True)
-    arrived = lax.all_gather(landed[None], "mic", axis=0, tiled=True)
+    own = landed[None]
+    size = lax.axis_size("mic")
+    forward = [(i, (i + 1) % size) for i in range(size)]
+    terms = [own]
+    for hop in range(1, size):
+        terms = [lax.ppermute(terms[0], "mic", forward), *terms]
+    whole = jnp.concatenate(terms, axis=0)
+    turn = (lax.axis_index("mic") + 1) * terms[-1].shape[0]
+    arrived = jnp.roll(whole, turn, axis=0)
     flat = arrived.reshape(mic_count * seq_count * exp_local * capacity, model_width)
     piece_rows = flat.reshape(-1, exp_local, capacity, model_width)
     first_proj = jnp.einsum(

time: 347 us -> 370 us (1.066)
  waiting for transfers between devices: 201 us -> 218 us
  local copies, waits for them, and re-layouts: 36.6 us -> 44.4 us
    ppermute x0 -> x3, waiting for transfers between devices: none -> 54 us  [body(): terms = [lax.ppermute(terms[0], 'mic', forward), *terms]]
    all_gather x1 -> x0, waiting for transfers between devices: 37.7 us -> none  [body(): arrived = lax.all_gather(landed[None], 'mic', axis=0, tiled=True)]
    unnamed x18 -> x25, local copies, waits for them, and re-layouts: 1.2 us -> 6.54 us
  transfers between devices with their start and end apart: 5 -> 7, of which waited for: 5 -> 7; matrix products, arithmetic and copies ran while one was open for 11% -> 10% of each run, Pallas kernels for 0% -> 0%
where the time goes in v1:
time: 370 us; the launch traced here: 369 us
  waiting for transfers between devices  218 us (59%)
  local copies, waits for them, and re-layouts  44.4 us (12%)
  matrix products  39.8 us (11%)
  blocking collectives  35.1 us (9%)
  starting transfers between devices  16 us (4%)
  between operations  13.7 us (4%)
    all_gather x1, waiting for transfers between devices, body(): lax.all_gather(w_join, ('mic', 'seq'), axis=0, tiled=True)  59.9 us
    ppermute x3, waiting for transfers between devices, body(): terms = [lax.ppermute(terms[0], 'mic', forward), *terms]  54 us
    reduce_scatter x1, waiting for transfers between devices, body(): lax.psum_scatter(result.reshape(lax.axis_size('mic') * (seq_count * exp_l...  41.6 us
    all_to_all x1, waiting for transfers between devices, body(): lax.all_to_all(projected, 'mic', split_axis=1, concat_axis=0, tiled=True)  35.4 us
    all_to_all x1, blocking collectives, body(): lax.all_to_all(buffers, 'seq', split_axis=0, concat_axis=0, tiled=True)  35.1 us
    all_to_all x1, waiting for transfers between devices, body(): lax.all_to_all(summed, 'seq', split_axis=0, concat_axis=0, tiled=True)  26.5 us
    convert_element_type x2, local copies, waits for them, and re-layouts, body(): summed = lax.psum_scatter(result.reshape(lax.axis_size('mic') * (seq_coun...  11.9 us
    dot_general x1, matrix products, body(): jnp.einsum('nejf,efd->nejd', inner, w_down, preferred_element_type=jnp.fl...  11.3 us
  transfers between devices with their start and end apart: 7, of which 7 were waited for; matrix products, arithmetic and copies ran while one was open for 10% of the time, Pallas kernels for 0%

profile of v1, /device:TPU:1, one launch (start us, length us, event | category | flops | bytes accessed | tf_op | source)
XLA Modules:
  0.0 369.4 jit_solution(3145688667992886278)
XLA Ops:
  6.5 0.0 copy-start
  6.5 0.0 all-gather.2.cloned.1.call-start
  6.5 0.7 all-gather.2.cloned.1.call-update
  7.3 1.2 copy-done
  8.4 3.0 convolution_convert_fusion
  11.5 2.0 copy.26
  13.4 5.1 %all-to-all-start = ((bf16[2,4,128,1536]{3,2,0,1:T(8,128)(2,1)}), bf16[2,4,128,1536]{3,2,0,1:T(8,128)(2,1)S(1)}, u32[]{:S(2)}, u32[]{:S(2)}) async-start(bf16[2,4,128,1536]{3,2,0,1:T(8,128)(2,1)} %copy.26), calls=%async_computation | async-start | bytes 6291456 | tf_op jit(solution)/shard_map/all_to_all | solution.py:25
  18.6 0.0 reduce-scatter.2.cloned.1.call-start
  18.6 0.0 copy-done.7
  18.6 0.1 copy.35
  18.7 0.2 reduce_window_sum.11
  18.9 0.1 copy.37
  19.1 0.1 copy.38
  19.2 35.4 %all-to-all-done = bf16[2,4,128,1536]{3,2,0,1:T(8,128)(2,1)S(1)} async-done(((bf16[2,4,128,1536]{3,2,0,1:T(8,128)(2,1)}), bf16[2,4,128,1536]{3,2,0,1:T(8,128)(2,1)S(1)}, u32[]{:S(2)}, u32[]{:S(2)}) %all-to-all-start) | async-done | bytes 3145760 | tf_op jit(solution)/shard_map/all_to_all | solution.py:25
  54.6 1.9 fusion.37
  56.5 1.7 copy.28
  58.2 0.0 copy-start.3
  58.2 3.7 %copy.30 = bf16[8,128,8,64]{3,0,2,1:T(8,128)(2,1)} copy(bf16[8,128,8,64]{1,3,2,0:T(8,128)(2,1)S(1)} %bitcast.108) | data formatting | bytes 2097152 | tf_op jit(solution)/shard_map/reshape | solution.py:28
  62.0 0.0 copy-done.4
  62.0 0.7 copy.29
  62.6 3.7 %copy.31 = bf16[8,128,8,64]{3,0,2,1:T(8,128)(2,1)} copy(bf16[8,128,8,64]{1,3,2,0:T(8,128)(2,1)S(1)} %bitcast.109) | data formatting | bytes 2097152 | tf_op jit(solution)/shard_map/reshape | solution.py:29
  66.4 0.0 copy-done.3
  66.4 0.7 copy.27
  67.0 3.0 copy.32
  70.0 7.2 %fusion.38 = (f32[128,8,8]{2,1,0:T(8,128)S(1)}, f32[128,8,8,8]{2,3,1,0:T(8,128)}) fusion(bf16[8,128,8,64]{3,0,2,1:T(8,128)(2,1)} %copy.30, bf16[8,128,8,64]{3,0,2,1:T(8,128)(2,1)} %copy.31), kind=kOutput, calls=%fused_computation.65 | convolution fusion | flops 8585223 | bytes 2392064 | tf_op jit(solution)/shard_map/sub | solution.py:37
  77.2 4.2 %convert_bitcast_fusion.1 = bf16[128,8,8,64]{3,1,2,0:T(8,128)(2,1)} fusion(bf16[8,128,8,64]{3,0,2,1:T(8,128)(2,1)S(1)} %copy.32, f32[128,8,8,8]{2,3,1,0:T(8,128)} %get-tuple-element.11, f32[128,8,8]{2,1,0:T(8,128)S(1)} %get-tuple-element.10), kind=kOutput, calls=%fused_computation.22 | convolution fusion | flops 9043968 | bytes 2392064 | tf_op jit(solution)/shard_map/fhij,jfhd->fihd/dot_general | solution.py:39
  81.4 3.2 copy.34
  84.6 59.9 %all-gather.2.cloned.1.call-done = bf16[4096,1024]{1,0:T(8,128)(2,1)} async-done(((bf16[16,1024]{1,0:T(8,128)(2,1)}), bf16[4096,1024]{1,0:T(8,128)(2,1)}) %all-gather.2.cloned.1.call-update) | async-done | bytes 8388624 | tf_op jit(solution)/shard_map/all_gather | solution.py:45
  144.5 4.7 %multiply_reduce_fusion.1 = (f32[128]{0:T(128)S(1)}, f32[128,1024]{1,0:T(8,128)S(1)}) fusion(bf16[128,4096]{0,1:T(8,128)(2,1)S(1)} %bitcast.107, bf16[4096,1024]{1,0:T(8,128)(2,1)} %all-gather.2.cloned.1.call-done), kind=kOutput, calls=%fused_computation.39 | convolution fusion | flops 1074003840 | bytes 9961984 | tf_op jit(solution)/shard_map/dot_general | solution.py:43
  149.3 0.4 convolution_convert_fusion.1
  149.8 0.3 copy-done.2
  150.1 0.3 reshape.92
  150.4 35.1 %all_to_all.25 = bf16[64,6,1024]{2,1,0:T(8,128)(2,1)S(1)} all-to-all(bf16[64,6,1024]{2,1,0:T(8,128)(2,1)S(1)} %reshape.92), channel_id=1, replica_groups=mesh['mic'=4,'seq'=64] {'seq'}, dimensions={0} | all-to-all | bytes 1572864 | tf_op jit(solution)/shard_map/all_to_all | solution.py:70
  185.4 0.4 copy.39
  185.9 0.1 collective-permute-start
  186.0 18.9 %collective-permute-done = bf16[1,64,6,1024]{3,1,2,0:T(8,128)(2,1)S(1)} collective-permute-done((bf16[1,64,6,1024]{3,1,2,0:T(8,128)(2,1)S(1)}, bf16[1,64,6,1024]{3,1,2,0:T(8,128)(2,1)S(1)}, u32[]{:S(2)}, u32[]{:S(2)}) %collective-permute-start) | collective-permute-done | bytes 786464 | tf_op jit(solution)/shard_map/ppermute | solution.py:76
  204.8 0.0 collective-permute-start.1
  204.8 18.0 %collective-permute-done.1 = bf16[1,64,6,1024]{3,1,2,0:T(8,128)(2,1)S(1)} collective-permute-done((bf16[1,64,6,1024]{3,1,2,0:T(8,128)(2,1)S(1)}, bf16[1,64,6,1024]{3,1,2,0:T(8,128)(2,1)S(1)}, u32[]{:S(2)}, u32[]{:S(2)}) %collective-permute-start.1) | collective-permute-done | bytes 786464 | tf_op jit(solution)/shard_map/ppermute | solution.py:76
  222.8 0.0 collective-permute-start.2
  222.8 17.1 %collective-permute-done.2 = bf16[1,64,6,1024]{3,1,2,0:T(8,128)(2,1)} collective-permute-done((bf16[1,64,6,1024]{3,1,2,0:T(8,128)(2,1)S(1)}, bf16[1,64,6,1024]{3,1,2,0:T(8,128)(2,1)}, u32[]{:S(2)}, u32[]{:S(2)}) %collective-permute-start.2) | collective-permute-done | bytes 786464 | tf_op jit(solution)/shard_map/ppermute | solution.py:76
  240.0 1.6 copy_dynamic-update-slice_fusion.4
  241.5 0.4 copy_dynamic-update-slice_fusion.2
  242.0 0.4 copy_dynamic-update-slice_fusion
  242.4 0.1 constant_dynamic-update-slice_fusion.1
  242.5 1.6 copy_dynamic-update-slice_fusion.5
  244.1 0.4 copy_dynamic-update-slice_fusion.3
  244.5 0.4 copy_dynamic-update-slice_fusion.1
  245.0 0.1 constant_dynamic-update-slice_fusion
  245.1 0.4 constant_dynamic-slice_fusion
  245.5 0.0 copy-start.8
  245.5 1.7 copy.46
  247.3 5.3 %fusion.19 = f32[256,6,1024]{2,0,1:T(8,128)} fusion(bf16[256,6,1024]{2,0,1:T(8,128)(2,1)S(1)} %bitcast.111, bf16[1,1024,1024]{2,1,0:T(8,128)(2,1)S(1)} %copy-done.8), kind=kOutput, calls=%fused_computation.20 | convolution fusion | flops 3221225472 | bytes 11534336 | tf_op jit(solution)/shard_map/nejd,edf->nejf/dot_general | solution.py:82
  252.6 11.3 %convert_bitcast_fusion = bf16[256,1,6,1024]{3,0,2,1:T(8,128)(2,1)} fusion(f32[256,6,1024]{2,0,1:T(8,128)} %fusion.19, bf16[256,6,1024]{2,0,1:T(8,128)(2,1)S(1)} %bitcast.112, bf16[1,1024,1024]{2,1,0:T(8,128)(2,1)} %param.16, bf16[1,1024,1024]{2,1,0:T(8,128)(2,1)} %param.15), kind=kOutput, calls=%fused_computation.15 | convolution fusion | flops 6453460992 | bytes 16777216 | tf_op jit(solution)/shard_map/nejf,efd->nejd/dot_general | solution.py:87
  263.9 5.6 %copy.47 = bf16[256,1,6,1024]{3,2,0,1:T(8,128)(2,1)} copy(bf16[256,1,6,1024]{3,0,2,1:T(8,128)(2,1)} %convert_bitcast_fusion) | data formatting | bytes 6291456 | tf_op jit(solution)/shard_map/convert_element_type | solution.py:91
  269.5 6.3 %convert_element_type.71 = bf16[1536,1024]{1,0:T(8,128)(2,1)} reshape(bf16[256,1,6,1024]{3,2,0,1:T(8,128)(2,1)} %copy.47) | data formatting | bytes 6291456 | tf_op jit(solution)/shard_map/convert_element_type | solution.py:91
  275.8 0.0 reduce-scatter.2.cloned.1.call-update
  275.9 0.0 copy-start.1
  275.9 41.6 %reduce-scatter.2.cloned.1.call-done = bf16[384,1024]{1,0:T(8,128)(2,1)} async-done(((bf16[1536,1024]{1,0:T(8,128)(2,1)}), bf16[384,1024]{1,0:T(8,128)(2,1)}) %reduce-scatter.2.cloned.1.call-update) | async-done | bytes 786448 | tf_op jit(solution)/shard_map/reduce_scatter | solution.py:88
  317.5 2.2 reshape.98
  319.7 10.8 %all-to-all-start.2 = ((bf16[64,6,1024]{2,1,0:T(8,128)(2,1)}), bf16[64,6,1024]{2,1,0:T(8,128)(2,1)}, u32[]{:S(2)}, u32[]{:S(2)}) async-start(bf16[64,6,1024]{2,1,0:T(8,128)(2,1)} %reshape.98), calls=%async_computation.3 | async-start | bytes 2097152 | tf_op jit(solution)/shard_map/all_to_all | solution.py:97
  330.5 1.3 fusion.36
  331.9 26.5 %all-to-all-done.2 = bf16[64,6,1024]{2,1,0:T(8,128)(2,1)} async-done(((bf16[64,6,1024]{2,1,0:T(8,128)(2,1)}), bf16[64,6,1024]{2,1,0:T(8,128)(2,1)}, u32[]{:S(2)}, u32[]{:S(2)}) %all-to-all-start.2) | async-done | bytes 786464 | tf_op jit(solution)/shard_map/all_to_all | solution.py:97
  358.4 2.3 fusion.24
  360.7 1.8 fusion.28
  (20 shorter events, 0.3 us)
Async XLA Ops:
  6.5 1.9 copy-start
  6.5 138.0 %all-gather.2.cloned.1.call-start = ((), (), s32[]{:S(2)}) async-start(), calls=%async_computation.4 | async-start | bytes 8421376 | tf_op jit(solution)/shard_map/all_gather | solution.py:45
  13.4 5.2 %copy-start.7 = (s32[1,1,128,2]{2,3,1,0:T(2,128)S(1)}, s32[1,1,128,2]{2,3,1,0:T(2,128)}, u32[]{:S(2)}) copy-start(s32[1,1,128,2]{2,3,1,0:T(2,128)} %param.17) | copy-start | bytes 3076
  13.4 41.2 %all-to-all-start = ((bf16[2,4,128,1536]{3,2,0,1:T(8,128)(2,1)}), bf16[2,4,128,1536]{3,2,0,1:T(8,128)(2,1)S(1)}, u32[]{:S(2)}, u32[]{:S(2)}) async-start(bf16[2,4,128,1536]{3,2,0,1:T(8,128)(2,1)} %copy.26), calls=%async_computation | async-start | bytes 6291456 | tf_op jit(solution)/shard_map/all_to_all | solution.py:25
  18.6 298.9 %reduce-scatter.2.cloned.1.call-start = ((), (), s32[]{:S(2)}) async-start(), calls=%async_computation.5 | async-start | bytes 3932160 | tf_op jit(solution)/shard_map/reduce_scatter | solution.py:88
  56.5 5.5 %copy-start.4 = (bf16[8,128,512]{2,1,0:T(8,128)(2,1)S(1)}, bf16[8,128,512]{2,1,0:T(8,128)(2,1)}, u32[]{:S(2)}) copy-start(bf16[8,128,512]{2,1,0:T(8,128)(2,1)} %get-tuple-element.7) | copy-start | bytes 3145732
  58.2 8.1 %copy-start.3 = (bf16[8,128,512]{2,1,0:T(8,128)(2,1)S(1)}, bf16[8,128,512]{2,1,0:T(8,128)(2,1)}, u32[]{:S(2)}) copy-start(bf16[8,128,512]{2,1,0:T(8,128)(2,1)} %get-tuple-element.9) | copy-start | bytes 3145732
  144.5 4.8 %copy-start.6 = (f32[1024]{0:T(1024)S(1)}, f32[1024]{0:T(1024)}, u32[]{:S(2)}) copy-start(f32[1024]{0:T(1024)} %param.12) | copy-start | bytes 12292
  149.3 0.8 copy-start.2
  185.9 19.0 %collective-permute-start = (bf16[1,64,6,1024]{3,1,2,0:T(8,128)(2,1)S(1)}, bf16[1,64,6,1024]{3,1,2,0:T(8,128)(2,1)S(1)}, u32[]{:S(2)}, u32[]{:S(2)}) collective-permute-start(bf16[1,64,6,1024]{3,1,2,0:T(8,128)(2,1)S(1)} %copy.39), channel_id=1, source_target_pairs={{0,64},{64,128},{128,192},{192,0},{1,65},{65,129},{129,193},{193,1... | collective-permute-start | bytes 2359304 | tf_op jit(solution)/shard_map/ppermute | solution.py:76
  204.8 18.0 %collective-permute-start.1 = (bf16[1,64,6,1024]{3,1,2,0:T(8,128)(2,1)S(1)}, bf16[1,64,6,1024]{3,1,2,0:T(8,128)(2,1)S(1)}, u32[]{:S(2)}, u32[]{:S(2)}) collective-permute-start(bf16[1,64,6,1024]{3,1,2,0:T(8,128)(2,1)S(1)} %collective-permute-done), channel_id=1, source_target_pairs={{0,64},{64,128},{128,192},{192,0},{1,65},{65,129},{129,193},{193,1... | collective-permute-start | bytes 2359304 | tf_op jit(solution)/shard_map/ppermute | solution.py:76
  222.8 17.1 %collective-permute-start.2 = (bf16[1,64,6,1024]{3,1,2,0:T(8,128)(2,1)S(1)}, bf16[1,64,6,1024]{3,1,2,0:T(8,128)(2,1)}, u32[]{:S(2)}, u32[]{:S(2)}) collective-permute-start(bf16[1,64,6,1024]{3,1,2,0:T(8,128)(2,1)S(1)} %collective-permute-done.1), channel_id=1, source_target_pairs={{0,64},{64,128},{128,192},{192,0},{1,65},{65,129},{129,193},{193,1... | collective-permute-start | bytes 2359304 | tf_op jit(solution)/shard_map/ppermute | solution.py:76
  245.5 1.7 copy-start.8
  275.8 54.7 %copy-start.5 = (bf16[1024,64]{0,1:T(8,128)(2,1)S(1)}, bf16[1024,64]{0,1:T(8,128)(2,1)}, u32[]{:S(2)}) copy-start(bf16[1024,64]{0,1:T(8,128)(2,1)} %param.13) | copy-start | bytes 393220
  275.9 86.7 %copy-start.1 = (bf16[2,512,1536]{2,1,0:T(8,128)(2,1)S(1)}, bf16[2,512,1536]{2,1,0:T(8,128)(2,1)}, u32[]{:S(2)}) copy-start(bf16[2,512,1536]{2,1,0:T(8,128)(2,1)} %param.10) | copy-start | bytes 9437188
  319.7 38.7 %all-to-all-start.2 = ((bf16[64,6,1024]{2,1,0:T(8,128)(2,1)}), bf16[64,6,1024]{2,1,0:T(8,128)(2,1)}, u32[]{:S(2)}, u32[]{:S(2)}) async-start(bf16[64,6,1024]{2,1,0:T(8,128)(2,1)} %reshape.98), calls=%async_computation.3 | async-start | bytes 2097152 | tf_op jit(solution)/shard_map/all_to_all | solution.py:97
Sparse Core Ops, SparseCore 0:
  10.9 133.5 all-gather.1
  276.0 41.4 reduce-scatter.1
